TPU v7x, 1024 devices: a whole 8x8x8 slice. The times are simulated.
1024 devices in a mesh: ctx: 16 (over y, core), uly: 64 (over x, z).
Axes of the slice: x: 8, y: 8, z: 8, core: 2. Of those that a mesh axis runs over, the one named last changes fastest.
Arguments:
- queries: bfloat16 [98304, 4096], P(('ctx', 'uly')), may hold values from -6 to 6
- keys: bfloat16 [98304, 4096], P(('ctx', 'uly')), may hold values from -6 to 6
- values: bfloat16 [98304, 4096], P(('ctx', 'uly')), may hold values from -6 to 6
- doc_ids: int32 [98304], P(('ctx', 'uly')), may hold values from 0 to 31, never falling along the last dimension, each value on 1 to 12288 neighbouring positions
- decay_rate: float32 [64], P('uly'), may hold values from 8.138021e-06 to 0.05
- norm_gain: float32 [4096], replicated, may hold values from 0.1 to 1.9
Outputs:
- attended: bfloat16 [98304, 4096], P(('ctx', 'uly'))
Inputs may be any that keep to these rules, and one draw needn't show every extreme that they name: doc_ids never fall along the sequence; every document has 1 to 12288 tokens and one has exactly that many.
All inputs are finite; a program needn't handle non-finite values.
Results may differ from a plain program's by a relative error of at most 0.0034.
Values may be sent and summed in bfloat16 or wider, within the bound.
A program may use at most 32 MiB of HBM per device.

v0:
```python
import jax
import jax.numpy as jnp
from jax import lax
from jax.sharding import PartitionSpec as P

HD = 64
BLK = 256


def from_behind(value, axis, steps):
    count = lax.axis_size(axis)
    first, last = (max(0, -steps), min(count, count - steps))
    return lax.ppermute(value, axis, [(source, source + steps) for source in range(first, last)])


def state_pass(keys3, values3, ids, rate, blk, start_state, start_last):
    length, heads, width = keys3.shape
    count = length // blk
    kblocks = keys3.reshape(count, blk, heads, width)
    vblocks = values3.reshape(count, blk, heads, width)
    iblocks = ids.reshape(count, blk)
    position = jnp.arange(blk).astype(jnp.float32)

    def advance(carry, pieces):
        state, last = carry
        kblock, vblock, iblock = pieces
        endid = iblock[blk - 1]
        keep = jnp.where(endid == last, jnp.exp(-rate * blk), jnp.float32(0.0))
        weights = jnp.where(
            (iblock == endid)[None, :],
            jnp.exp(-rate[:, None] * (blk - 1 - position)[None, :]),
            jnp.float32(0.0),
        )
        scaled = kblock.astype(jnp.float32) * jnp.transpose(weights)[:, :, None]
        fresh = jnp.einsum(
            "shd,she->hde", scaled, vblock.astype(jnp.float32), precision=lax.Precision.HIGHEST
        )
        return ((keep[:, None, None] * state + fresh, endid), (state, last))

    final, entries = lax.scan(advance, (start_state, start_last), (kblocks, vblocks, iblocks))
    return (final, entries)


def block_output(qblock, kblock, vblock, iblock, state, last, rate):
    blk = qblock.shape[0]
    position = jnp.arange(blk).astype(jnp.float32)
    q32 = qblock.astype(jnp.float32)
    scores = jnp.einsum("thd,shd->hts", qblock, kblock, preferred_element_type=jnp.float32)
    diff = position[:, None] - position[None, :]
    mask = (diff >= 0) & (iblock[:, None] == iblock[None, :])
    weight = jnp.where(
        mask[None], jnp.exp(-rate[:, None, None] * jnp.maximum(diff, 0.0)[None]), jnp.float32(0.0)
    )
    probs = (scores * weight).astype(jnp.bfloat16)
    intra = jnp.einsum("hts,shd->thd", probs, vblock, preferred_element_type=jnp.float32)
    factor = (
        jnp.exp(-rate[None, :] * (position + 1.0)[:, None])
        * (iblock == last).astype(jnp.float32)[:, None]
    )
    inter = (
        jnp.einsum("thd,hde->the", q32, state, precision=lax.Precision.HIGHEST) * factor[:, :, None]
    )
    return intra + inter


def combine_with(rate):

    def combine(earlier, later):
        state_one, count_one, last_one = earlier
        state_two, count_two, last_two = later
        linked = (count_two == 0.0) | (last_one == last_two)
        factor = jnp.where(linked, jnp.exp(-rate * count_two), jnp.float32(0.0))
        merged = state_two + factor[:, None, None] * state_one
        return (merged, count_one + count_two, jnp.where(count_two > 0.0, last_two, last_one))

    return combine


def fetch_queries(queries):
    return lax.all_to_all(queries, "uly", split_axis=1, concat_axis=0, tiled=True)


def local(queries, keys, values, doc_ids, decay_rate, norm_gain):
    heads_here = decay_rate.shape[0]
    slice_ids = lax.all_gather(doc_ids, "uly", axis=0, tiled=True)
    length = slice_ids.shape[0]
    k_here, v_here = (
        lax.all_to_all(keys, "uly", split_axis=1, concat_axis=0, tiled=True),
        lax.all_to_all(values, "uly", split_axis=1, concat_axis=0, tiled=True),
    )
    q_here = fetch_queries(queries)
    k3 = k_here.reshape(length, heads_here, HD)
    v3 = v_here.reshape(length, heads_here, HD)
    zero_state = jnp.zeros((heads_here, HD, HD), jnp.float32)
    final, entries = state_pass(k3, v3, slice_ids, decay_rate, BLK, zero_state, jnp.int32(-1))
    element = (final[0], jnp.float32(length), final[1].astype(jnp.float32))
    combine = combine_with(decay_rate)

    def relay(step, incoming):
        return from_behind(combine(incoming, element), "ctx", 1)

    start = (zero_state, jnp.float32(0.0), jnp.float32(0.0))
    carried = lax.fori_loop(0, lax.axis_size("ctx") - 1, relay, start)
    q3 = q_here.reshape(length, heads_here, HD)
    count = length // BLK
    states, lasts = entries

    def one(pieces):
        qblock, kblock, vblock, iblock, state, last = pieces
        return block_output(qblock, kblock, vblock, iblock, state, last, decay_rate)

    raw = lax.map(
        one,
        (
            q3.reshape(count, BLK, heads_here, HD),
            k3.reshape(count, BLK, heads_here, HD),
            v3.reshape(count, BLK, heads_here, HD),
            slice_ids.reshape(count, BLK),
            states,
            lasts,
        ),
    )
    raw = raw.reshape(length, heads_here, HD)
    carry_state, carry_count, carry_last = carried
    position = jnp.arange(length).astype(jnp.float32)
    factor = (
        jnp.exp(-decay_rate[None, :] * (position + 1.0)[:, None])
        * (slice_ids.astype(jnp.float32) == carry_last).astype(jnp.float32)[:, None]
    )
    raw = (
        raw
        + jnp.einsum(
            "thd,hde->the", q3.astype(jnp.float32), carry_state, precision=lax.Precision.HIGHEST
        )
        * factor[:, :, None]
    )
    total_width = norm_gain.shape[0]
    partial_sq = jnp.sum(raw * raw, axis=(1, 2))
    total_sq = lax.psum(partial_sq, "uly")
    scale = lax.rsqrt(total_sq / total_width + 1e-06)
    gain_here = lax.dynamic_slice_in_dim(
        norm_gain, lax.axis_index("uly") * (heads_here * HD), heads_here * HD
    )
    normed = (raw * scale[:, None, None] * gain_here.reshape(1, heads_here, HD)).astype(
        jnp.bfloat16
    )
    return lax.all_to_all(
        normed.reshape(length, heads_here * HD), "uly", split_axis=0, concat_axis=1, tiled=True
    )


def solution(mesh):
    in_specs = (
        P(("ctx", "uly"), None),
        P(("ctx", "uly"), None),
        P(("ctx", "uly"), None),
        P(("ctx", "uly")),
        P("uly"),
        P(),
    )
    out_specs = P(("ctx", "uly"), None)
    return jax.shard_map(local, mesh=mesh, in_specs=in_specs, out_specs=out_specs, check_vma=False)
```

profile of v0, /device:TPU:68, one launch (start us, length us, event | category | flops | bytes accessed | tf_op | source)
XLA Modules:
  0.0 1057.0 jit_solution(9753139642069936680)
XLA Ops:
  2.3 22.7 %all-to-all-start.1 = ((bf16[96,64,64]{0,2,1:T(8,128)(2,1)}), bf16[96,64,64]{0,2,1:T(8,128)(2,1)S(1)}, u32[]{:S(2)}, u32[]{:S(2)}) async-start(bf16[96,64,64]{0,2,1:T(8,128)(2,1)} %bitcast.16), calls=%async_computation.1 | async-start | bytes 2097152 | tf_op jit(solution)/shard_map/all_to_all | solution.py:80
  26.3 29.2 %all-to-all-done.1 = bf16[96,64,64]{0,2,1:T(8,128)(2,1)S(1)} async-done(((bf16[96,64,64]{0,2,1:T(8,128)(2,1)}), bf16[96,64,64]{0,2,1:T(8,128)(2,1)S(1)}, u32[]{:S(2)}, u32[]{:S(2)}) %all-to-all-start.1) | async-done | bytes 786464 | tf_op jit(solution)/shard_map/all_to_all | solution.py:80
  55.5 5.6 all-to-all-start.2
  62.4 28.8 %all-to-all-done.2 = bf16[96,64,64]{0,2,1:T(8,128)(2,1)S(1)} async-done(((bf16[96,64,64]{0,2,1:T(8,128)(2,1)}), bf16[96,64,64]{0,2,1:T(8,128)(2,1)S(1)}, u32[]{:S(2)}, u32[]{:S(2)}) %all-to-all-start.2) | async-done | bytes 786464 | tf_op jit(solution)/shard_map/all_to_all | solution.py:88
  91.2 5.7 all-to-all-start
  99.9 267.7 %all-reduce = s32[6144]{0:T(1024)S(1)} all-reduce(s32[6144]{0:T(1024)S(1)} %dynamic-update-slice), channel_id=1, replica_groups=mesh['ctx'=16,'uly'=64] {'uly'}, use_global_device_ids=true, to_apply=%add | all-reduce | flops 6144 | bytes 49152
  379.7 96.5 %while.47 = (s32[]{:T(128)}, f32[1,64,64]{2,1,0:T(8,128)S(1)}, s32[]{:T(128)}, f32[24,1,64,64]{3,2,1,0:T(8,128)}, s32[24]{0:T(128)S(1)}, /*index=5*/s32[24,256]{...) while((s32[]{:T(128)}, f32[1,64,64]{2,1,0:T(8,128)S(1)}, ...), condition=%wide.region_1.2_spmd.clone, body=%wide.region_0.1_spmd.clone.sunk | while | flops 12633350 | bytes 496886 | solution.py:40
  479.1 144.1 %while.45 = (s32[]{:T(128)}, f32[24,256,1,64]{1,0,3,2:T(8,128)}, bf16[24,256,1,64]{1,3,2,0:T(8,128)(2,1)S(1)}, bf16[24,256,1,64]{1,3,2,0:T(8,128)(2,1)}, bf16[24...) while((s32[]{:T(128)}, f32[24,256,1,64]{1,0,3,2:T(8,128)}, ...), condition=%wide.region_3.4_spmd, body=%wide.region_2.3_spmd.sunk | while | flops 29984256 | bytes 636057 | solution.py:112
  624.8 96.6 %while.46 = (s32[]{:T(128)}, f32[1,64,64]{2,1,0:T(8,128)S(1)}, f32[]{:T(128)}, f32[]{:T(128)}, f32[1]{0:T(128)}, /*index=5*/f32[1,64,64]{2,1,0:T(8,128)S(1)}, f32[]{:T(128)}, s32[]{:T(128)}, f32[1]{0:T(128)}) while((s32[]{:T(128)}, f32[1,64,64]{2,1,0:T(8,128)S(1)}, f32[]{:T(128)}, f32[]{:T(128)}, f32[1]{0:T(128)}, ...), condition=%wide.region_5.6_spmd, body=%wide.region_4.5_spmd.sunk | while | flops 8196 | bytes 114855 | solution.py:103
  633.8 3.9 collective-permute-done
  640.2 3.9 collective-permute-done
  646.7 3.9 collective-permute-done
  653.1 3.9 collective-permute-done
  659.6 3.9 collective-permute-done
  666.0 3.9 collective-permute-done
  672.4 3.9 collective-permute-done
  678.9 3.9 collective-permute-done
  685.3 3.9 collective-permute-done
  691.8 3.9 collective-permute-done
  698.2 3.9 collective-permute-done
  704.6 3.9 collective-permute-done
  711.1 3.9 collective-permute-done
  723.6 281.4 %psum.7 = f32[6144]{0:T(1024)S(1)} all-reduce(f32[6144]{0:T(1024)S(1)} %get-tuple-element.458), channel_id=1, replica_groups=mesh['ctx'=16,'uly'=64] {'uly'}, use_global_device_ids=true, to_apply=%region_7.8 | all-reduce | flops 6144 | bytes 49152 | tf_op jit(solution)/shard_map/psum | solution.py:139
  1008.8 47.0 %all_to_all.67 = bf16[64,96,64]{1,2,0:T(8,128)(2,1)S(1)} all-to-all(bf16[64,96,64]{1,2,0:T(8,128)(2,1)S(1)} %copy.39), channel_id=1, replica_groups=mesh['ctx'=16,'uly'=64] {'uly'}, dimensions={0} | all-to-all | bytes 1572864 | tf_op jit(solution)/shard_map/all_to_all | solution.py:147
  (480 shorter events, 274.6 us)
Async XLA Ops:
  0.0 25.0 %copy-start = (bf16[96,4096]{1,0:T(8,128)(2,1)S(1)}, bf16[96,4096]{1,0:T(8,128)(2,1)}, u32[]{:S(2)}) copy-start(bf16[96,4096]{1,0:T(8,128)(2,1)} %param.13) | copy-start | bytes 2359300
  2.3 53.2 %all-to-all-start.1 = ((bf16[96,64,64]{0,2,1:T(8,128)(2,1)}), bf16[96,64,64]{0,2,1:T(8,128)(2,1)S(1)}, u32[]{:S(2)}, u32[]{:S(2)}) async-start(bf16[96,64,64]{0,2,1:T(8,128)(2,1)} %bitcast.16), calls=%async_computation.1 | async-start | bytes 2097152 | tf_op jit(solution)/shard_map/all_to_all | solution.py:80
  25.0 36.1 %copy-start.1 = (bf16[96,4096]{1,0:T(8,128)(2,1)S(1)}, bf16[96,4096]{1,0:T(8,128)(2,1)}, u32[]{:S(2)}) copy-start(bf16[96,4096]{1,0:T(8,128)(2,1)} %param.14) | copy-start | bytes 2359300
  55.5 35.7 %all-to-all-start.2 = ((bf16[96,64,64]{0,2,1:T(8,128)(2,1)}), bf16[96,64,64]{0,2,1:T(8,128)(2,1)S(1)}, u32[]{:S(2)}, u32[]{:S(2)}) async-start(bf16[96,64,64]{0,2,1:T(8,128)(2,1)} %bitcast.18), calls=%async_computation.2 | async-start | bytes 2097152 | tf_op jit(solution)/shard_map/all_to_all | solution.py:88
  61.1 38.5 %copy-start.2 = (s32[96]{0:T(128)S(1)}, s32[96]{0:T(128)}, u32[]{:S(2)}) copy-start(s32[96]{0:T(128)} %param.15) | copy-start | bytes 1156
  91.2 284.9 %all-to-all-start = ((bf16[96,64,64]{0,2,1:T(8,128)(2,1)}), bf16[96,64,64]{0,2,1:T(8,128)(2,1)}, u32[]{:S(2)}, u32[]{:S(2)}) async-start(bf16[96,64,64]{0,2,1:T(8,128)(2,1)} %bitcast.14), calls=%async_computation | async-start | bytes 2097152 | tf_op jit(solution)/shard_map/all_to_all | solution.py:89
  476.2 148.5 %collective-permute-start.1 = (f32[]{:T(128)}, f32[]{:T(128)}, u32[]{:S(2)}, u32[]{:S(2)}) collective-permute-start(f32[]{:T(128)} %convert_element_type.79), channel_id=1, source_target_pairs={{0,64},{64,128},{128,192},{192,256},{256,320},{320,384},{384,448},... | collective-permute-start | bytes 20 | tf_op jit(solution)/shard_map/while/body/eval_jaxpr/ppermute | solution.py:13
  624.8 6.4 collective-permute-start
  631.2 6.4 collective-permute-start
  637.7 6.4 collective-permute-start
  644.1 6.4 collective-permute-start
  650.6 6.4 collective-permute-start
  657.0 6.4 collective-permute-start
  663.4 6.4 collective-permute-start
  669.9 6.4 collective-permute-start
  676.3 6.4 collective-permute-start
  682.8 6.4 collective-permute-start
  689.2 6.4 collective-permute-start
  695.6 6.4 collective-permute-start
  702.1 6.4 collective-permute-start
  708.5 6.4 collective-permute-start
  715.0 6.4 collective-permute-start
where the time goes:
time: 1060 us
  blocking collectives  596 us (56%)
  local copies, waits for them, and re-layouts  122 us (12%)
  waiting for transfers between devices  116 us (11%)
  starting transfers between devices  66.1 us (6%)
  matrix products  61.4 us (6%)
  other arithmetic  51.5 us (5%)
  loops' own time  42.5 us (4%)
    psum x1, blocking collectives, local(): total_sq = lax.psum(partial_sq, 'uly')  281 us
    unnamed x1, blocking collectives  268 us
    dynamic_update_slice x48, local copies, waits for them, and re-layouts, local(): lax.map(one, (q3.reshape(count, BLK, heads_here, HD), k3.reshape(count, B...  60 us
    ppermute x16, waiting for transfers between devices, from_behind(): lax.ppermute(value, axis, [(source, source + steps) for source in range(f...  57.5 us
    all_to_all x1, blocking collectives, local(): lax.all_to_all(normed.reshape(length, heads_here * HD), 'uly', split_axis...  47 us
    ppermute x16, starting transfers between devices, from_behind(): lax.ppermute(value, axis, [(source, source + steps) for source in range(f...  32.2 us
    another operation x1, loops' own time, state_pass(): lax.scan(advance, (start_state, start_last), (kblocks, vblocks, iblocks))  32.1 us
    all_to_all x1, waiting for transfers between devices, fetch_queries(): lax.all_to_all(queries, 'uly', split_axis=1, concat_axis=0, tiled=True)  29.2 us
  transfers between devices with their start and end apart: 19, of which 17 were waited for; matrix products, arithmetic and copies ran while one was open for 15% of the time, Pallas kernels for 0%

commit v1 on v0

v1 whole, which is shorter than its diff:
```python
import functools
import math
import jax
import jax.numpy as jnp
from jax import lax
from jax.experimental import pallas as pl
from jax.experimental.pallas import tpu as pltpu
from jax.sharding import PartitionSpec as P

HD = 64
PAIR = 2 * HD
F32 = jnp.float32
BF16 = jnp.bfloat16
MESH = pl.DeviceIdType.MESH
CONTRACT_ROWS = (((0,), (0,)), ((), ()))
CONTRACT_LANES = (((1,), (1,)), ((), ()))
PLAIN = (((1,), (0,)), ((), ()))
FAR = -1e30


def dot(a, b, dims):
    return lax.dot_general(a, b, dims, preferred_element_type=F32)


def kernel(nx, nz, nctx, tok, q_hbm, k_hbm, v_hbm, ids_ref, rate_ref, gain_ref, out_ref,
           q_ref, k_ref, v_ref, info, negdiff, doc, raw, sumsq,
           s_send, s_recv, line, t_recv, u_buf, c_send, c1_recv, c2_recv, o_send, o_recv,
           p_send, p_recv, prev_row,
           load_sem, iz_s, iz_r, ix_s, ix_r, s_s, s_r, t_s, t_r, c_s, c_r, o_s, o_r, p_s, p_r):
    n = nx * nz
    chunks = nx // 2
    rx = HD // nx
    slab = nz * tok
    ctx = lax.axis_index("ctx")
    me = lax.axis_index("uly")
    x, z = me // nz, me % nz

    loads = [pltpu.make_async_copy(a, b, load_sem.at[i])
             for i, (a, b) in enumerate(((k_hbm, k_ref), (v_hbm, v_ref), (q_hbm, q_ref)))]
    for load in loads:
        load.start()
    barrier = pltpu.get_barrier_semaphore()

    def on_line(off):
        return (z + off) % nz

    def on_column(off):
        return (x + off) % nx

    def dev(xx, zz):
        return (ctx, xx * nz + zz)

    def later(steps):
        return ((ctx + steps + nctx) % nctx, me)

    def greet_z(off, _):
        pl.semaphore_signal(barrier, inc=1, device_id=dev(x, on_line(off)), device_id_type=MESH)
        return 0

    def greet_x(off, _):
        pl.semaphore_signal(barrier, inc=1, device_id=dev(on_column(off), z), device_id_type=MESH)
        return 0

    lax.fori_loop(1, nz, greet_z, 0)
    lax.fori_loop(1, nx, greet_x, 0)
    for steps in (1, 2, -1, -2):
        pl.semaphore_signal(barrier, inc=1, device_id=later(steps), device_id_type=MESH)

    ids = ids_ref[...].astype(F32)
    last = jnp.max(ids, axis=1, keepdims=True)
    sub = lax.broadcasted_iota(jnp.int32, (8, PAIR), 0)
    info[me] = jnp.where(sub < 4, jnp.full((8, PAIR), rate_ref[0], F32),
                         jnp.broadcast_to(last, (8, PAIR)))
    t_at = lax.broadcasted_iota(jnp.int32, (tok, tok), 0)
    s_at = lax.broadcasted_iota(jnp.int32, (tok, tok), 1)
    ids_all = jnp.broadcast_to(ids, (tok, tok))
    column = jnp.sum(jnp.where(t_at == s_at, ids_all, 0.0), axis=1, keepdims=True)
    negdiff[...] = jnp.where((t_at >= s_at) & (column == ids_all), (s_at - t_at).astype(F32), FAR)
    doc[...] = jnp.broadcast_to(column, (tok, PAIR))
    sumsq[...] = jnp.zeros_like(sumsq)
    pl.semaphore_wait(barrier, nz + nx - 2 + 4)

    def info_z(to, frm):
        return pltpu.make_async_remote_copy(info.at[frm], info.at[frm], iz_s.at[to % nz], iz_r.at[frm % nz],
                                            device_id=(ctx, to), device_id_type=MESH)

    def info_x(xto, xfrm):
        rows = info.at[pl.ds(xfrm * nz, nz)]
        return pltpu.make_async_remote_copy(rows, rows, ix_s.at[xto], ix_r.at[xfrm],
                                            device_id=dev(xto, z), device_id_type=MESH)

    def loop_z(body):
        def step(off, _):
            body(on_line(off))
            return 0
        lax.fori_loop(1, nz, step, 0)

    def loop_x(body):
        def step(off, _):
            body(on_column(off))
            return 0
        lax.fori_loop(1, nx, step, 0)

    loop_z(lambda zz: info_z(x * nz + zz, me).start())
    loop_z(lambda zz: info_z(me, x * nz + zz).wait_recv())
    loop_x(lambda xx: info_x(xx, x).start())
    for load in loads:
        load.wait()
    loop_x(lambda xx: info_x(x, xx).wait_recv())

    low = lax.broadcasted_iota(jnp.int32, (1, PAIR), 1) < HD
    mask_low = jnp.where(low, 1.0, 0.0)
    keep_low = mask_low.astype(BF16)
    keep_high = (1.0 - mask_low).astype(BF16)

    def pair_rate(pair):
        return jnp.where(low, info[2 * pair, 0:1, :], info[2 * pair + 1, 0:1, :])

    def last_of(j):
        return info[j, 4:5, :]

    def pair_columns(pair):
        return pl.ds(pl.multiple_of(pair * PAIR, PAIR), PAIR)

    def join(big, rows):
        return jnp.where(low, big[:rows], big[rows:])

    after = (tok - 1 - lax.broadcasted_iota(jnp.int32, (tok, PAIR), 0)).astype(F32)
    after = jnp.where(doc[...] == last_of(me), -after, FAR)

    def end_state(pair):
        kp = k_ref[:, pair_columns(pair)].astype(F32) * jnp.exp(after * pair_rate(pair))
        vp = v_ref[:, pair_columns(pair)]
        high = kp.astype(BF16)
        rest = (kp - high.astype(F32)).astype(BF16)
        both = dot(jnp.concatenate([high, rest], 0), jnp.concatenate([vp, vp], 0), CONTRACT_ROWS)
        return join(both, HD).astype(BF16)

    def send_state(c, to, frm):
        return pltpu.make_async_remote_copy(s_send.at[c, to], s_recv.at[c, frm], s_s.at[c, to], s_r.at[c, frm],
                                            device_id=dev(x, to), device_id_type=MESH)

    for c in range(chunks):
        def state_out(zz, c=c):
            s_send[c, zz] = end_state(zz * chunks + c)
            send_state(c, zz, z).start()
        loop_z(state_out)
        s_recv[c, z] = end_state(z * chunks + c)

    def intra(pair, _):
        columns = pair_columns(pair)
        q2 = q_ref[:, columns]
        qq = jnp.concatenate([q2 * keep_low, q2 * keep_high], 0)
        scores = dot(qq, k_ref[:, columns], CONTRACT_LANES)
        gaps = negdiff[...]
        weight = jnp.concatenate([jnp.exp(gaps * info[2 * pair, 0:1, :tok]),
                                  jnp.exp(gaps * info[2 * pair + 1, 0:1, :tok])], 0)
        probs = (scores * weight).astype(BF16)
        raw[:, columns] = join(dot(probs, v_ref[:, columns], PLAIN), tok)
        return 0

    def send_total(c, to, frm):
        return pltpu.make_async_remote_copy(line.at[nz, c, pl.ds(pl.multiple_of(to * rx, rx), rx)], t_recv.at[c, frm],
                                            t_s.at[c, to], t_r.at[c, frm],
                                            device_id=dev(to, z), device_id_type=MESH)

    def scan_line(c):
        loop_z(lambda zz: send_state(c, z, zz).wait_recv())
        decay = jnp.exp(-float(tok) * pair_rate(z * chunks + c))
        total = jnp.zeros((HD, PAIR), F32)
        for zz in range(nz):
            line[zz, c] = total
            state = s_recv[c, zz].astype(F32)
            if zz:
                here = last_of(x * nz + zz)
                state = state + jnp.where(here == last_of(x * nz + zz - 1), decay, 0.0) * total
            total = state
        line[nz, c] = total
        t_recv[c, x] = line[nz, c, pl.ds(pl.multiple_of(x * rx, rx), rx)]
        loop_x(lambda xx: send_total(c, xx, x).start())

    def send_slice(c, steps):
        land, i = ((c1_recv, 0), (c2_recv, 1))[steps - 1]
        return pltpu.make_async_remote_copy(c_send.at[c], land.at[c], c_s.at[c, i], c_r.at[c, i],
                                            device_id=later(steps), device_id_type=MESH)

    def scan_lines(c):
        loop_x(lambda xx: send_total(c, x, xx).wait_recv())
        decay = jnp.exp(-float(slab) * pair_rate(z * chunks + c))
        total = jnp.zeros((rx, PAIR), F32)
        for xx in range(nx):
            u_buf[c, xx] = total
            state = t_recv[c, xx]
            if xx:
                linked = last_of(xx * nz + nz - 1) == last_of(xx * nz - 1)
                state = state + jnp.where(linked, decay, 0.0) * total
            total = state
        c_send[c, 0:rx] = total
        c_send[c, rx:rx + 8] = jnp.broadcast_to(last_of(n - 1), (8, PAIR))
        send_slice(c, 1).start()
        send_slice(c, 2).start()

    def send_carry(c, to, frm):
        return pltpu.make_async_remote_copy(o_send.at[c, to], o_recv.at[c, frm], o_s.at[c, to], o_r.at[c, frm],
                                            device_id=dev(to, z), device_id_type=MESH)

    def carry_lines(c):
        send_slice(c, 1).wait_recv()
        send_slice(c, 2).wait_recv()
        rate = pair_rate(z * chunks + c)
        one, two = c1_recv[c, 0:rx], c2_recv[c, 0:rx]
        last_one, last_two = c1_recv[c, rx:rx + 1], c2_recv[c, rx:rx + 1]
        reach = jnp.where((ctx >= 2) & (last_one == last_two), jnp.exp(-float(slab * nx) * rate), 0.0)
        carry = jnp.where(ctx >= 1, one + reach * two, 0.0)
        before = jnp.where(ctx >= 1, last_one, -1.0)
        if c == 0:
            prev_row[...] = jnp.broadcast_to(before, (8, PAIR))
        for xx in range(nx):
            value = u_buf[c, xx]
            if xx:
                linked = last_of(xx * nz - 1) == before
                value = value + jnp.where(linked, jnp.exp(-float(slab * xx) * rate), 0.0) * carry
            else:
                value = value + carry
            o_send[c, xx] = value
        o_recv[c, x] = o_send[c, x]
        loop_x(lambda xx: send_carry(c, xx, x).start())

    def send_prefix(c, to, frm):
        return pltpu.make_async_remote_copy(p_send.at[c, to], p_recv.at[c, frm], p_s.at[c, to], p_r.at[c, frm],
                                            device_id=dev(x, to), device_id_type=MESH)

    def before_line():
        return jnp.where(x == 0, prev_row[0:1], last_of((me - z + n - 1) % n))

    def prefixes(c):
        loop_x(lambda xx: send_carry(c, x, xx).wait_recv())
        rate = pair_rate(z * chunks + c)
        before = before_line()

        def prefix(zz):
            linked = (zz == 0) | (last_of((x * nz + zz + n - 1) % n) == before)
            reach = jnp.where(linked, jnp.exp(-float(tok) * zz.astype(F32) * rate), 0.0)
            return (line[zz, c] + reach * o_recv[c].reshape(HD, PAIR)).astype(BF16)

        def prefix_out(zz):
            p_send[c, zz] = prefix(zz)
            send_prefix(c, zz, z).start()

        loop_z(prefix_out)
        p_recv[c, z] = prefix(z)

    upto = -(1 + lax.broadcasted_iota(jnp.int32, (tok, PAIR), 0)).astype(F32)

    def finish(c):
        before = jnp.where(z == 0, before_line(), last_of((me + n - 1) % n))
        gaps = jnp.where(doc[...] == before, upto, FAR)

        def add(zz):
            pair = zz * chunks + c
            columns = pair_columns(pair)
            state = p_recv[c, zz]
            wide = jnp.concatenate([state * keep_low, state * keep_high], 0)
            inter = dot(q_ref[:, columns], wide, PLAIN)
            value = raw[:, columns] + inter * jnp.exp(gaps * pair_rate(pair))
            raw[:, columns] = value
            sumsq[...] += value * value

        add(z)

        def arrived(zz):
            send_prefix(c, z, zz).wait_recv()
            add(zz)
        loop_z(arrived)

    pairs = n // 2
    steps = chunks + 5
    done = 0
    for step in range(steps):
        want = min(pairs, (pairs * (step + 1) + 5) // 6)
        if want > done:
            lax.fori_loop(done, want, intra, 0)
            done = want
        if step < chunks:
            scan_line(step)
        if 0 <= step - 2 < chunks:
            scan_lines(step - 2)
        if 0 <= step - 3 < chunks:
            carry_lines(step - 3)
        if 0 <= step - 5 < chunks:
            prefixes(step - 5)
    for c in range(chunks):
        finish(c)

    width = n * HD
    mean = jnp.sum(sumsq[...], axis=1, keepdims=True) * (1.0 / width)
    scale = jnp.broadcast_to(lax.rsqrt(mean + 1e-6), (tok, PAIR))

    def write(pair, _):
        columns = pair_columns(pair)
        out_ref[:, columns] = (raw[:, columns] * scale * gain_ref[0:1, columns]).astype(BF16)
        return 0
    lax.fori_loop(0, pairs, write, 0)

    loop_z(lambda zz: info_z(x * nz + zz, me).wait_send())
    loop_x(lambda xx: info_x(xx, x).wait_send())
    for c in range(chunks):
        loop_z(lambda zz: send_state(c, zz, z).wait_send())
        loop_x(lambda xx: send_total(c, xx, x).wait_send())
        send_slice(c, 1).wait_send()
        send_slice(c, 2).wait_send()
        loop_x(lambda xx: send_carry(c, xx, x).wait_send())
        loop_z(lambda zz: send_prefix(c, zz, z).wait_send())


def solution(mesh, nz=None):
    nctx, n = mesh.shape["ctx"], mesh.shape["uly"]
    nz = nz or math.isqrt(n)
    nx = n // nz
    chunks, rx = nx // 2, HD // nx

    def local(queries, keys, values, doc_ids, decay_rate, norm_gain):
        tok, width = queries.shape
        vmem = pl.BlockSpec(memory_space=pltpu.VMEM)
        anywhere = pl.BlockSpec(memory_space=pl.ANY)
        sem = pltpu.SemaphoreType.DMA
        return pl.pallas_call(
            functools.partial(kernel, nx, nz, nctx, tok),
            out_shape=jax.ShapeDtypeStruct((tok, width), BF16),
            in_specs=[anywhere, anywhere, anywhere, vmem, pl.BlockSpec(memory_space=pltpu.SMEM), vmem],
            out_specs=vmem,
            scratch_shapes=[
                pltpu.VMEM((tok, width), BF16),
                pltpu.VMEM((tok, width), BF16),
                pltpu.VMEM((tok, width), BF16),
                pltpu.VMEM((n, 8, PAIR), F32),
                pltpu.VMEM((tok, tok), F32),
                pltpu.VMEM((tok, PAIR), F32),
                pltpu.VMEM((tok, width), F32),
                pltpu.VMEM((tok, PAIR), F32),
                pltpu.VMEM((chunks, nz, HD, PAIR), BF16),
                pltpu.VMEM((chunks, nz, HD, PAIR), BF16),
                pltpu.VMEM((nz + 1, chunks, HD, PAIR), F32),
                pltpu.VMEM((chunks, nx, rx, PAIR), F32),
                pltpu.VMEM((chunks, nx, rx, PAIR), F32),
                pltpu.VMEM((chunks, rx + 8, PAIR), F32),
                pltpu.VMEM((chunks, rx + 8, PAIR), F32),
                pltpu.VMEM((chunks, rx + 8, PAIR), F32),
                pltpu.VMEM((chunks, nx, rx, PAIR), F32),
                pltpu.VMEM((chunks, nx, rx, PAIR), F32),
                pltpu.VMEM((chunks, nz, HD, PAIR), BF16),
                pltpu.VMEM((chunks, nz, HD, PAIR), BF16),
                pltpu.VMEM((8, PAIR), F32),
                sem((3,)),
                sem((nz,)), sem((nz,)), sem((nx,)), sem((nx,)),
                sem((chunks, nz)), sem((chunks, nz)),
                sem((chunks, nx)), sem((chunks, nx)),
                sem((chunks, 2)), sem((chunks, 2)),
                sem((chunks, nx)), sem((chunks, nx)),
                sem((chunks, nz)), sem((chunks, nz)),
            ],
            compiler_params=pltpu.CompilerParams(collective_id=0, has_side_effects=True,
                                                 vmem_limit_bytes=48 * 1024 * 1024),
        )(queries, keys, values, doc_ids.reshape(1, tok), decay_rate, norm_gain.reshape(1, width))

    rows = P(("ctx", "uly"), None)
    return jax.shard_map(local, mesh=mesh,
                         in_specs=(rows, rows, rows, P(("ctx", "uly")), P("uly"), P()),
                         out_specs=rows, check_vma=False)
```

time: 1060 us -> 81 us (0.08)
  the two profiles are of different devices: /device:TPU:68 before, /device:TPU:2 now
where the time goes in v1:
time: 81 us; the launch traced here: 80.6 us
  Pallas kernels  74.3 us (92%)
  local copies, waits for them, and re-layouts  5.65 us (7%)
    pallas_call x1, Pallas kernels, local(): pl.pallas_call(functools.partial(kernel, nx, nz, nctx, tok), out_shape=ja...  74.3 us
    unnamed x11, local copies, waits for them, and re-layouts  5.65 us

profile of v1, /device:TPU:2, one launch (start us, length us, event | category | flops | bytes accessed | tf_op | source)
XLA Modules:
  0.0 80.6 jit_solution(1838675790311906850)
XLA Ops:
  0.7 0.0 copy-start.4
  0.7 0.6 copy-done.4
  1.3 0.0 copy-start
  1.3 1.1 %copy-done = bf16[96,4096]{1,0:T(8,128)(2,1)S(1)} copy-done((bf16[96,4096]{1,0:T(8,128)(2,1)S(1)}, bf16[96,4096]{1,0:T(8,128)(2,1)}, u32[]{:S(2)}) %copy-start) | copy-done | bytes 786456
  2.4 0.0 copy-start.1
  2.4 1.1 %copy-done.1 = bf16[96,4096]{1,0:T(8,128)(2,1)S(1)} copy-done((bf16[96,4096]{1,0:T(8,128)(2,1)S(1)}, bf16[96,4096]{1,0:T(8,128)(2,1)}, u32[]{:S(2)}) %copy-start.1) | copy-done | bytes 786456
  3.6 0.0 copy-start.2
  3.6 1.1 %copy-done.2 = bf16[96,4096]{1,0:T(8,128)(2,1)S(1)} copy-done((bf16[96,4096]{1,0:T(8,128)(2,1)S(1)}, bf16[96,4096]{1,0:T(8,128)(2,1)}, u32[]{:S(2)}) %copy-start.2) | copy-done | bytes 786456
  4.7 0.0 copy-start.3
  4.7 0.7 copy-done.3
  5.4 74.3 %shard_map.64 = bf16[96,4096]{1,0:T(8,128)(2,1)S(1)} custom-call(bf16[96,4096]{1,0:T(8,128)(2,1)S(1)} %copy-done, bf16[96,4096]{1,0:T(8,128)(2,1)S(1)} %copy-done.1, bf16[96,4096]{1,0:T(8,128)(2,1)S(1)} %copy-done.2, s32[1,96]{1,0:T(1,128)S(1)} %bitcast.3, f32[1]{0:T(128)S(6)} %copy.8.rate_ref, f32[1,4096]{1,0:T(1,128)S(1)} %bitcast.2), custom_call_target="tpu_custom_call" | custom-call | tf_op jit(solution)/shard_map/pallas_call | solution.py:327
  79.8 0.9 %copy.9 = bf16[96,4096]{1,0:T(8,128)(2,1)} copy(bf16[96,4096]{1,0:T(8,128)(2,1)S(1)} %shard_map.64) | data formatting | bytes 1572864
Async XLA Ops:
  0.7 0.7 copy-start.4
  1.3 1.1 %copy-start = (bf16[96,4096]{1,0:T(8,128)(2,1)S(1)}, bf16[96,4096]{1,0:T(8,128)(2,1)}, u32[]{:S(2)}) copy-start(bf16[96,4096]{1,0:T(8,128)(2,1)} %q_hbm.1) | copy-start | bytes 2359300
  2.4 1.1 %copy-start.1 = (bf16[96,4096]{1,0:T(8,128)(2,1)S(1)}, bf16[96,4096]{1,0:T(8,128)(2,1)}, u32[]{:S(2)}) copy-start(bf16[96,4096]{1,0:T(8,128)(2,1)} %k_hbm.1) | copy-start | bytes 2359300
  3.6 1.1 %copy-start.2 = (bf16[96,4096]{1,0:T(8,128)(2,1)S(1)}, bf16[96,4096]{1,0:T(8,128)(2,1)}, u32[]{:S(2)}) copy-start(bf16[96,4096]{1,0:T(8,128)(2,1)} %v_hbm.1) | copy-start | bytes 2359300
  4.7 0.7 copy-start.3

commit v2 on v1

--- a/solution.py
+++ b/solution.py
@@ -22,8 +22,8 @@
     return lax.dot_general(a, b, dims, preferred_element_type=F32)
 
 
-def kernel(nx, nz, nctx, tok, q_hbm, k_hbm, v_hbm, ids_ref, rate_ref, gain_ref, out_ref,
-           q_ref, k_ref, v_ref, info, negdiff, doc, raw, sumsq,
+def kernel(nx, nz, nctx, tok, q_hbm, k_hbm, v_hbm, ids_hbm, gain_hbm, rate_ref, out_ref,
+           ids_ref, gain_ref, q_ref, k_ref, v_ref, k_turned, scores, info, negdiff, doc, raw, sumsq,
            s_send, s_recv, line, t_recv, u_buf, c_send, c1_recv, c2_recv, o_send, o_recv,
            p_send, p_recv, prev_row,
            load_sem, iz_s, iz_r, ix_s, ix_r, s_s, s_r, t_s, t_r, c_s, c_r, o_s, o_r, p_s, p_r):
@@ -36,9 +36,7 @@
     x, z = me // nz, me % nz
 
     loads = [pltpu.make_async_copy(a, b, load_sem.at[i])
-             for i, (a, b) in enumerate(((k_hbm, k_ref), (v_hbm, v_ref), (q_hbm, q_ref)))]
-    for load in loads:
-        load.start()
+             for i, (a, b) in enumerate(((ids_hbm, ids_ref), (k_hbm, k_ref), (v_hbm, v_ref), (q_hbm, q_ref), (gain_hbm, gain_ref)))]
     barrier = pltpu.get_barrier_semaphore()
 
     def on_line(off):
@@ -65,12 +63,14 @@
     lax.fori_loop(1, nx, greet_x, 0)
     for steps in (1, 2, -1, -2):
         pl.semaphore_signal(barrier, inc=1, device_id=later(steps), device_id_type=MESH)
-
+    for load in loads:
+        load.start()
+
+    loads[0].wait()
     ids = ids_ref[...].astype(F32)
     last = jnp.max(ids, axis=1, keepdims=True)
-    sub = lax.broadcasted_iota(jnp.int32, (8, PAIR), 0)
-    info[me] = jnp.where(sub < 4, jnp.full((8, PAIR), rate_ref[0], F32),
-                         jnp.broadcast_to(last, (8, PAIR)))
+    info[me] = jnp.where(lax.broadcasted_iota(jnp.int32, (2, PAIR), 0) < 1, jnp.full((2, PAIR), rate_ref[0], F32),
+                         jnp.broadcast_to(last, (2, PAIR)))
     t_at = lax.broadcasted_iota(jnp.int32, (tok, tok), 0)
     s_at = lax.broadcasted_iota(jnp.int32, (tok, tok), 1)
     ids_all = jnp.broadcast_to(ids, (tok, tok))
@@ -101,63 +101,78 @@
             return 0
         lax.fori_loop(1, nx, step, 0)
 
-    loop_z(lambda zz: info_z(x * nz + zz, me).start())
-    loop_z(lambda zz: info_z(me, x * nz + zz).wait_recv())
-    loop_x(lambda xx: info_x(xx, x).start())
-    for load in loads:
-        load.wait()
-    loop_x(lambda xx: info_x(x, xx).wait_recv())
-
     low = lax.broadcasted_iota(jnp.int32, (1, PAIR), 1) < HD
     mask_low = jnp.where(low, 1.0, 0.0)
     keep_low = mask_low.astype(BF16)
     keep_high = (1.0 - mask_low).astype(BF16)
 
+    def pair_columns(pair):
+        return pl.ds(pl.multiple_of(pair * PAIR, PAIR), PAIR)
+
+    pairs = n // 2
+
+    def over_pairs(first, end, width, body):
+        def step(i, _):
+            for j in range(width):
+                body(first + i * width + j)
+            return 0
+        lax.fori_loop(0, (end - first) // width, step, 0)
+
+    def turn(pair):
+        k_turned[pair] = k_ref[:, pair_columns(pair)].astype(F32).T
+
+    def score(pair):
+        q2 = q_ref[:, pair_columns(pair)]
+        qq = jnp.concatenate([q2 * keep_low, q2 * keep_high], 0)
+        scores[pair] = dot(qq, k_ref[:, pair_columns(pair)], CONTRACT_LANES)
+
+    loop_z(lambda zz: info_z(x * nz + zz, me).start())
+    loads[1].wait()
+    over_pairs(0, pairs, 4, turn)
+    loop_z(lambda zz: info_z(me, x * nz + zz).wait_recv())
+    loop_x(lambda xx: info_x(xx, x).start())
+    for load in loads[2:]:
+        load.wait()
+    over_pairs(0, pairs, 4, score)
+    loop_x(lambda xx: info_x(x, xx).wait_recv())
+
     def pair_rate(pair):
         return jnp.where(low, info[2 * pair, 0:1, :], info[2 * pair + 1, 0:1, :])
 
     def last_of(j):
-        return info[j, 4:5, :]
-
-    def pair_columns(pair):
-        return pl.ds(pl.multiple_of(pair * PAIR, PAIR), PAIR)
+        return info[j, 1:2, :]
 
     def join(big, rows):
         return jnp.where(low, big[:rows], big[rows:])
 
-    after = (tok - 1 - lax.broadcasted_iota(jnp.int32, (tok, PAIR), 0)).astype(F32)
-    after = jnp.where(doc[...] == last_of(me), -after, FAR)
+    after = (tok - 1 - lax.broadcasted_iota(jnp.int32, (1, tok), 1)).astype(F32)
+    after = jnp.where(ids == last, -after, FAR)
 
     def end_state(pair):
-        kp = k_ref[:, pair_columns(pair)].astype(F32) * jnp.exp(after * pair_rate(pair))
+        turned = k_turned[pair]
+        kp = jnp.concatenate([turned[:HD] * jnp.exp(after * info[2 * pair, 0:1, :tok]),
+                              turned[HD:] * jnp.exp(after * info[2 * pair + 1, 0:1, :tok])], 0)
         vp = v_ref[:, pair_columns(pair)]
         high = kp.astype(BF16)
         rest = (kp - high.astype(F32)).astype(BF16)
-        both = dot(jnp.concatenate([high, rest], 0), jnp.concatenate([vp, vp], 0), CONTRACT_ROWS)
-        return join(both, HD).astype(BF16)
+        return join(dot(high, vp, PLAIN) + dot(rest, vp, PLAIN), HD).astype(BF16)
 
     def send_state(c, to, frm):
         return pltpu.make_async_remote_copy(s_send.at[c, to], s_recv.at[c, frm], s_s.at[c, to], s_r.at[c, frm],
                                             device_id=dev(x, to), device_id_type=MESH)
 
     for c in range(chunks):
-        def state_out(zz, c=c):
-            s_send[c, zz] = end_state(zz * chunks + c)
-            send_state(c, zz, z).start()
-        loop_z(state_out)
+        for off in range(1, nz):
+            s_send[c, on_line(off)] = end_state(on_line(off) * chunks + c)
+        loop_z(lambda zz: send_state(c, zz, z).start())
         s_recv[c, z] = end_state(z * chunks + c)
 
-    def intra(pair, _):
-        columns = pair_columns(pair)
-        q2 = q_ref[:, columns]
-        qq = jnp.concatenate([q2 * keep_low, q2 * keep_high], 0)
-        scores = dot(qq, k_ref[:, columns], CONTRACT_LANES)
+    def intra(pair):
         gaps = negdiff[...]
         weight = jnp.concatenate([jnp.exp(gaps * info[2 * pair, 0:1, :tok]),
                                   jnp.exp(gaps * info[2 * pair + 1, 0:1, :tok])], 0)
-        probs = (scores * weight).astype(BF16)
-        raw[:, columns] = join(dot(probs, v_ref[:, columns], PLAIN), tok)
-        return 0
+        probs = (scores[pair] * weight).astype(BF16)
+        raw[:, pair_columns(pair)] = join(dot(probs, v_ref[:, pair_columns(pair)], PLAIN), tok)
 
     def send_total(c, to, frm):
         return pltpu.make_async_remote_copy(line.at[nz, c, pl.ds(pl.multiple_of(to * rx, rx), rx)], t_recv.at[c, frm],
@@ -256,39 +271,29 @@
         before = jnp.where(z == 0, before_line(), last_of((me + n - 1) % n))
         gaps = jnp.where(doc[...] == before, upto, FAR)
 
-        def add(zz):
+        loop_z(lambda zz: send_prefix(c, z, zz).wait_recv())
+        total = sumsq[...]
+        for zz in range(nz):
             pair = zz * chunks + c
-            columns = pair_columns(pair)
             state = p_recv[c, zz]
             wide = jnp.concatenate([state * keep_low, state * keep_high], 0)
-            inter = dot(q_ref[:, columns], wide, PLAIN)
-            value = raw[:, columns] + inter * jnp.exp(gaps * pair_rate(pair))
-            raw[:, columns] = value
-            sumsq[...] += value * value
-
-        add(z)
-
-        def arrived(zz):
-            send_prefix(c, z, zz).wait_recv()
-            add(zz)
-        loop_z(arrived)
-
-    pairs = n // 2
-    steps = chunks + 5
+            inter = dot(q_ref[:, pair * PAIR:(pair + 1) * PAIR], wide, PLAIN)
+            value = raw[:, pair * PAIR:(pair + 1) * PAIR] + inter * jnp.exp(gaps * pair_rate(pair))
+            raw[:, pair * PAIR:(pair + 1) * PAIR] = value
+            total = total + value * value
+        sumsq[...] = total
+
+    stages = ((scan_line, 0.0), (scan_lines, 4.3), (carry_lines, 6.3), (prefixes, 10.6))
+    events = sorted((2.8 * c + lag, i, c) for i, (_, lag) in enumerate(stages) for c in range(chunks))
+    share = -(-pairs // max(1, len(events) - 4))
+    share += share % 2
     done = 0
-    for step in range(steps):
-        want = min(pairs, (pairs * (step + 1) + 5) // 6)
+    for place, (_, i, c) in enumerate(events):
+        want = min(pairs, share * (place + 1))
         if want > done:
-            lax.fori_loop(done, want, intra, 0)
+            over_pairs(done, want, 2, intra)
             done = want
-        if step < chunks:
-            scan_line(step)
-        if 0 <= step - 2 < chunks:
-            scan_lines(step - 2)
-        if 0 <= step - 3 < chunks:
-            carry_lines(step - 3)
-        if 0 <= step - 5 < chunks:
-            prefixes(step - 5)
+        stages[i][0](c)
     for c in range(chunks):
         finish(c)
 
@@ -296,11 +301,10 @@
     mean = jnp.sum(sumsq[...], axis=1, keepdims=True) * (1.0 / width)
     scale = jnp.broadcast_to(lax.rsqrt(mean + 1e-6), (tok, PAIR))
 
-    def write(pair, _):
+    def write(pair):
         columns = pair_columns(pair)
         out_ref[:, columns] = (raw[:, columns] * scale * gain_ref[0:1, columns]).astype(BF16)
-        return 0
-    lax.fori_loop(0, pairs, write, 0)
+    over_pairs(0, pairs, 4, write)
 
     loop_z(lambda zz: info_z(x * nz + zz, me).wait_send())
     loop_x(lambda xx: info_x(xx, x).wait_send())
@@ -322,18 +326,22 @@
     def local(queries, keys, values, doc_ids, decay_rate, norm_gain):
         tok, width = queries.shape
         vmem = pl.BlockSpec(memory_space=pltpu.VMEM)
-        anywhere = pl.BlockSpec(memory_space=pl.ANY)
+        anywhere = pl.BlockSpec(memory_space=pltpu.HBM)
         sem = pltpu.SemaphoreType.DMA
         return pl.pallas_call(
             functools.partial(kernel, nx, nz, nctx, tok),
             out_shape=jax.ShapeDtypeStruct((tok, width), BF16),
-            in_specs=[anywhere, anywhere, anywhere, vmem, pl.BlockSpec(memory_space=pltpu.SMEM), vmem],
+            in_specs=[anywhere] * 5 + [pl.BlockSpec(memory_space=pltpu.SMEM)],
             out_specs=vmem,
             scratch_shapes=[
+                pltpu.VMEM((1, tok), jnp.int32),
+                pltpu.VMEM((1, width), F32),
                 pltpu.VMEM((tok, width), BF16),
                 pltpu.VMEM((tok, width), BF16),
                 pltpu.VMEM((tok, width), BF16),
-                pltpu.VMEM((n, 8, PAIR), F32),
+                pltpu.VMEM((n // 2, PAIR, tok), F32),
+                pltpu.VMEM((n // 2, 2 * tok, tok), F32),
+                pltpu.VMEM((n, 2, PAIR), F32),
                 pltpu.VMEM((tok, tok), F32),
                 pltpu.VMEM((tok, PAIR), F32),
                 pltpu.VMEM((tok, width), F32),
@@ -351,7 +359,7 @@
                 pltpu.VMEM((chunks, nz, HD, PAIR), BF16),
                 pltpu.VMEM((chunks, nz, HD, PAIR), BF16),
                 pltpu.VMEM((8, PAIR), F32),
-                sem((3,)),
+                sem((5,)),
                 sem((nz,)), sem((nz,)), sem((nx,)), sem((nx,)),
                 sem((chunks, nz)), sem((chunks, nz)),
                 sem((chunks, nx)), sem((chunks, nx)),
@@ -361,7 +369,8 @@
             ],
             compiler_params=pltpu.CompilerParams(collective_id=0, has_side_effects=True,
                                                  vmem_limit_bytes=48 * 1024 * 1024),
-        )(queries, keys, values, doc_ids.reshape(1, tok), decay_rate, norm_gain.reshape(1, width))
+        )(*(pltpu.with_memory_space_constraint(a, pltpu.HBM)
+            for a in (queries, keys, values, doc_ids.reshape(1, tok), norm_gain.reshape(1, width))), decay_rate)
 
     rows = P(("ctx", "uly"), None)
     return jax.shard_map(local, mesh=mesh,

time: 81 us -> 72.6 us (0.90)
  local copies, waits for them, and re-layouts: 5.65 us -> 0.88 us
  Pallas kernels: 74.3 us -> 70.8 us
    unnamed x11 -> x1, local copies, waits for them, and re-layouts: 5.65 us -> 0.88 us
    pallas_call x1, Pallas kernels: 74.3 us -> 70.8 us  [local(): pl.pallas_call(functools.partial(kernel, nx, nz, nctx, tok), out_shape=ja...]
where the time goes in v2:
time: 72.6 us; the launch traced here: 72.4 us
  Pallas kernels  70.8 us (98%)
  local copies, waits for them, and re-layouts  0.88 us (1%)
    pallas_call x1, Pallas kernels, local(): pl.pallas_call(functools.partial(kernel, nx, nz, nctx, tok), out_shape=ja...  70.8 us

profile of v2, /device:TPU:2, one launch (start us, length us, event | category | flops | bytes accessed | tf_op | source)
XLA Modules:
  0.0 72.4 jit_solution(250773719109802502)
XLA Ops:
  0.7 70.8 %shard_map.64 = bf16[96,4096]{1,0:T(8,128)(2,1)S(1)} custom-call(bf16[96,4096]{1,0:T(8,128)(2,1)} %q_hbm.1, bf16[96,4096]{1,0:T(8,128)(2,1)} %k_hbm.1, bf16[96,4096]{1,0:T(8,128)(2,1)} %v_hbm.1, s32[1,96]{1,0:T(1,128)} %bitcast.3, f32[1,4096]{1,0:T(1,128)} %bitcast.2, f32[1]{0:T(128)S(6)} %copy.8.rate_ref), custom_call_target="tpu_custom_call" | custom-call | tf_op jit(solution)/shard_map/pallas_call | solution.py:331
  71.5 0.9 %copy.9 = bf16[96,4096]{1,0:T(8,128)(2,1)} copy(bf16[96,4096]{1,0:T(8,128)(2,1)S(1)} %shard_map.64) | data formatting | bytes 1572864

commit v3 on v2

--- a/solution.py
+++ b/solution.py
@@ -24,9 +24,9 @@
 
 def kernel(nx, nz, nctx, tok, q_hbm, k_hbm, v_hbm, ids_hbm, gain_hbm, rate_ref, out_ref,
            ids_ref, gain_ref, q_ref, k_ref, v_ref, k_turned, scores, info, negdiff, doc, raw, sumsq,
-           s_send, s_recv, line, t_recv, u_buf, c_send, c1_recv, c2_recv, o_send, o_recv,
-           p_send, p_recv, prev_row,
-           load_sem, iz_s, iz_r, ix_s, ix_r, s_s, s_r, t_s, t_r, c_s, c_r, o_s, o_r, p_s, p_r):
+           s_send, s_recv, line, t_recv, ends, ends_recv, o_send, o_recv,
+           p_send, p_recv,
+           load_sem, iz_s, iz_r, ix_s, ix_r, s_s, s_r, t_s, t_r, ready, e_s, e_r, o_s, o_r, p_s, p_r):
     n = nx * nz
     chunks = nx // 2
     rx = HD // nx
@@ -48,9 +48,6 @@
     def dev(xx, zz):
         return (ctx, xx * nz + zz)
 
-    def later(steps):
-        return ((ctx + steps + nctx) % nctx, me)
-
     def greet_z(off, _):
         pl.semaphore_signal(barrier, inc=1, device_id=dev(x, on_line(off)), device_id_type=MESH)
         return 0
@@ -61,8 +58,13 @@
 
     lax.fori_loop(1, nz, greet_z, 0)
     lax.fori_loop(1, nx, greet_x, 0)
-    for steps in (1, 2, -1, -2):
-        pl.semaphore_signal(barrier, inc=1, device_id=later(steps), device_id_type=MESH)
+    for k in (1, 2):
+        @pl.when(ctx + k < nctx)
+        def _():
+            def greet(xx, _):
+                pl.semaphore_signal(barrier, inc=1, device_id=(ctx + k, xx * nz + z), device_id_type=MESH)
+                return 0
+            lax.fori_loop(0, nx, greet, 0)
     for load in loads:
         load.start()
 
@@ -78,7 +80,10 @@
     negdiff[...] = jnp.where((t_at >= s_at) & (column == ids_all), (s_at - t_at).astype(F32), FAR)
     doc[...] = jnp.broadcast_to(column, (tok, PAIR))
     sumsq[...] = jnp.zeros_like(sumsq)
-    pl.semaphore_wait(barrier, nz + nx - 2 + 4)
+    for cond, slices in ((ctx == 0, 0), (ctx == 1, 1), (ctx >= 2, 2)):
+        @pl.when(cond)
+        def _():
+            pl.semaphore_wait(barrier, nz + nx - 2 + slices * nx)
 
     def info_z(to, frm):
         return pltpu.make_async_remote_copy(info.at[frm], info.at[frm], iz_s.at[to % nz], iz_r.at[frm % nz],
@@ -100,6 +105,18 @@
             body(on_column(off))
             return 0
         lax.fori_loop(1, nx, step, 0)
+
+    def far_z(body):
+        for off in sorted(range(1, nz), key=lambda o: -min(o, nz - o)):
+            body(on_line(off))
+
+    def every_x(body):
+        for off in sorted(range(nx), key=lambda o: -min(o, nx - o)):
+            body(on_column(off))
+
+    def far_x(body):
+        for off in sorted(range(1, nx), key=lambda o: -min(o, nx - o)):
+            body(on_column(off))
 
     low = lax.broadcasted_iota(jnp.int32, (1, PAIR), 1) < HD
     mask_low = jnp.where(low, 1.0, 0.0)
@@ -126,15 +143,33 @@
         qq = jnp.concatenate([q2 * keep_low, q2 * keep_high], 0)
         scores[pair] = dot(qq, k_ref[:, pair_columns(pair)], CONTRACT_LANES)
 
-    loop_z(lambda zz: info_z(x * nz + zz, me).start())
+    far_z(lambda zz: info_z(x * nz + zz, me).start())
+    for k in (1, 2):
+        @pl.when(ctx >= k)
+        def _():
+            def welcome(xx, _):
+                pl.semaphore_signal(ready.at[k - 1], inc=1, device_id=(ctx - k, xx * nz + z), device_id_type=MESH)
+                return 0
+            lax.fori_loop(0, nx, welcome, 0)
     loads[1].wait()
     over_pairs(0, pairs, 4, turn)
     loop_z(lambda zz: info_z(me, x * nz + zz).wait_recv())
-    loop_x(lambda xx: info_x(xx, x).start())
+    far_x(lambda xx: info_x(xx, x).start())
     for load in loads[2:]:
         load.wait()
     over_pairs(0, pairs, 4, score)
     loop_x(lambda xx: info_x(x, xx).wait_recv())
+
+    def send_ends(k):
+        return pltpu.make_async_remote_copy(ends, ends_recv.at[k - 1], e_s.at[k - 1], e_r.at[k - 1],
+                                            device_id=(ctx + k, me), device_id_type=MESH)
+
+    def when_later(k, body):
+        pl.when(ctx + k < nctx)(body)
+
+    def when_earlier(k, body):
+        pl.when(ctx >= k)(body)
+
 
     def pair_rate(pair):
         return jnp.where(low, info[2 * pair, 0:1, :], info[2 * pair + 1, 0:1, :])
@@ -161,11 +196,25 @@
         return pltpu.make_async_remote_copy(s_send.at[c, to], s_recv.at[c, frm], s_s.at[c, to], s_r.at[c, frm],
                                             device_id=dev(x, to), device_id_type=MESH)
 
+    ahead = 3
+
+    def state_out(c):
+        far_z(lambda zz: send_state(c, zz, z).start())
+
     for c in range(chunks):
         for off in range(1, nz):
             s_send[c, on_line(off)] = end_state(on_line(off) * chunks + c)
-        loop_z(lambda zz: send_state(c, zz, z).start())
+        if c < ahead:
+            state_out(c)
         s_recv[c, z] = end_state(z * chunks + c)
+
+    for xx in range(nx):
+        ends[xx:xx + 1, :] = last_of(xx * nz + nz - 1)
+    for k in (1, 2):
+        @pl.when(ctx + k < nctx)
+        def _():
+            pl.semaphore_wait(ready.at[k - 1], nx)
+            send_ends(k).start()
 
     def intra(pair):
         gaps = negdiff[...]
@@ -174,14 +223,20 @@
         probs = (scores[pair] * weight).astype(BF16)
         raw[:, pair_columns(pair)] = join(dot(probs, v_ref[:, pair_columns(pair)], PLAIN), tok)
 
-    def send_total(c, to, frm):
-        return pltpu.make_async_remote_copy(line.at[nz, c, pl.ds(pl.multiple_of(to * rx, rx), rx)], t_recv.at[c, frm],
-                                            t_s.at[c, to], t_r.at[c, frm],
-                                            device_id=dev(to, z), device_id_type=MESH)
+    def send_total(c, k, to, frm):
+        return pltpu.make_async_remote_copy(line.at[nz, c, pl.ds(pl.multiple_of(to * rx, rx), rx)],
+                                            t_recv.at[c, k, frm], t_s.at[c, k, to], t_r.at[c, k, frm],
+                                            device_id=(ctx + k, to * nz + z), device_id_type=MESH)
+
+    def all_x(body):
+        def step(xx, _):
+            body(xx)
+            return 0
+        lax.fori_loop(0, nx, step, 0)
 
     def scan_line(c):
+        decay = jnp.exp(-float(tok) * pair_rate(z * chunks + c))
         loop_z(lambda zz: send_state(c, z, zz).wait_recv())
-        decay = jnp.exp(-float(tok) * pair_rate(z * chunks + c))
         total = jnp.zeros((HD, PAIR), F32)
         for zz in range(nz):
             line[zz, c] = total
@@ -191,79 +246,64 @@
                 state = state + jnp.where(here == last_of(x * nz + zz - 1), decay, 0.0) * total
             total = state
         line[nz, c] = total
-        t_recv[c, x] = line[nz, c, pl.ds(pl.multiple_of(x * rx, rx), rx)]
-        loop_x(lambda xx: send_total(c, xx, x).start())
-
-    def send_slice(c, steps):
-        land, i = ((c1_recv, 0), (c2_recv, 1))[steps - 1]
-        return pltpu.make_async_remote_copy(c_send.at[c], land.at[c], c_s.at[c, i], c_r.at[c, i],
-                                            device_id=later(steps), device_id_type=MESH)
-
-    def scan_lines(c):
-        loop_x(lambda xx: send_total(c, x, xx).wait_recv())
-        decay = jnp.exp(-float(slab) * pair_rate(z * chunks + c))
-        total = jnp.zeros((rx, PAIR), F32)
-        for xx in range(nx):
-            u_buf[c, xx] = total
-            state = t_recv[c, xx]
-            if xx:
-                linked = last_of(xx * nz + nz - 1) == last_of(xx * nz - 1)
-                state = state + jnp.where(linked, decay, 0.0) * total
-            total = state
-        c_send[c, 0:rx] = total
-        c_send[c, rx:rx + 8] = jnp.broadcast_to(last_of(n - 1), (8, PAIR))
-        send_slice(c, 1).start()
-        send_slice(c, 2).start()
+        t_recv[c, 0, x] = line[nz, c, pl.ds(pl.multiple_of(x * rx, rx), rx)]
+        far_x(lambda xx: send_total(c, 0, xx, x).start())
+        for k in (1, 2):
+            when_later(k, lambda: every_x(lambda xx: send_total(c, k, xx, x).start()))
 
     def send_carry(c, to, frm):
         return pltpu.make_async_remote_copy(o_send.at[c, to], o_recv.at[c, frm], o_s.at[c, to], o_r.at[c, frm],
                                             device_id=dev(to, z), device_id_type=MESH)
 
-    def carry_lines(c):
-        send_slice(c, 1).wait_recv()
-        send_slice(c, 2).wait_recv()
-        rate = pair_rate(z * chunks + c)
-        one, two = c1_recv[c, 0:rx], c2_recv[c, 0:rx]
-        last_one, last_two = c1_recv[c, rx:rx + 1], c2_recv[c, rx:rx + 1]
-        reach = jnp.where((ctx >= 2) & (last_one == last_two), jnp.exp(-float(slab * nx) * rate), 0.0)
-        carry = jnp.where(ctx >= 1, one + reach * two, 0.0)
-        before = jnp.where(ctx >= 1, last_one, -1.0)
+    def end_of(k, xx):
+        return ends_recv[k - 1, xx:xx + 1, :] if k else last_of(xx * nz + nz - 1)
+
+    def scan_lines(c):
+        decay = jnp.exp(-float(slab) * pair_rate(z * chunks + c))
         if c == 0:
-            prev_row[...] = jnp.broadcast_to(before, (8, PAIR))
-        for xx in range(nx):
-            value = u_buf[c, xx]
-            if xx:
-                linked = last_of(xx * nz - 1) == before
-                value = value + jnp.where(linked, jnp.exp(-float(slab * xx) * rate), 0.0) * carry
-            else:
-                value = value + carry
-            o_send[c, xx] = value
+            for k in (1, 2):
+                when_earlier(k, lambda: send_ends(k).wait_recv())
+        for k in (2, 1):
+            when_earlier(k, lambda: all_x(lambda xx: send_total(c, k, x, xx).wait_recv()))
+        loop_x(lambda xx: send_total(c, 0, x, xx).wait_recv())
+        carry, before = jnp.zeros((rx, PAIR), F32), None
+        for k in (2, 1, 0):
+            for xx in range(nx):
+                here = end_of(k, xx)
+                if k == 0:
+                    o_send[c, xx] = carry
+                    if xx == nx - 1:
+                        break
+                fresh = t_recv[c, k, xx]
+                if k:
+                    fresh = jnp.where(ctx >= k, fresh, 0.0)
+                if before is not None:
+                    fresh = fresh + jnp.where(here == before, decay, 0.0) * carry
+                carry, before = fresh, here
         o_recv[c, x] = o_send[c, x]
-        loop_x(lambda xx: send_carry(c, xx, x).start())
+        far_x(lambda xx: send_carry(c, xx, x).start())
 
     def send_prefix(c, to, frm):
         return pltpu.make_async_remote_copy(p_send.at[c, to], p_recv.at[c, frm], p_s.at[c, to], p_r.at[c, frm],
                                             device_id=dev(x, to), device_id_type=MESH)
 
     def before_line():
-        return jnp.where(x == 0, prev_row[0:1], last_of((me - z + n - 1) % n))
+        slice_before = jnp.where(ctx >= 1, ends_recv[0, nx - 1:nx, :], -1.0)
+        return jnp.where(x == 0, slice_before, last_of((me - z + n - 1) % n))
 
     def prefixes(c):
-        loop_x(lambda xx: send_carry(c, x, xx).wait_recv())
         rate = pair_rate(z * chunks + c)
         before = before_line()
-
-        def prefix(zz):
-            linked = (zz == 0) | (last_of((x * nz + zz + n - 1) % n) == before)
-            reach = jnp.where(linked, jnp.exp(-float(tok) * zz.astype(F32) * rate), 0.0)
-            return (line[zz, c] + reach * o_recv[c].reshape(HD, PAIR)).astype(BF16)
-
-        def prefix_out(zz):
-            p_send[c, zz] = prefix(zz)
-            send_prefix(c, zz, z).start()
-
-        loop_z(prefix_out)
-        p_recv[c, z] = prefix(z)
+        reach = []
+        for zz in range(nz):
+            far = jnp.exp(-float(tok * zz) * rate)
+            reach.append(jnp.where(last_of(x * nz + zz - 1) == before, far, 0.0) if zz else far)
+        loop_x(lambda xx: send_carry(c, x, xx).wait_recv())
+        carry = o_recv[c].reshape(HD, PAIR)
+        for zz in range(nz):
+            p_send[c, zz] = (line[zz, c] + reach[zz] * carry).astype(BF16)
+        far_z(lambda zz: send_prefix(c, zz, z).start())
+        p_recv[c, z] = p_send[c, z]
 
     upto = -(1 + lax.broadcasted_iota(jnp.int32, (tok, PAIR), 0)).astype(F32)
 
@@ -283,17 +323,17 @@
             total = total + value * value
         sumsq[...] = total
 
-    stages = ((scan_line, 0.0), (scan_lines, 4.3), (carry_lines, 6.3), (prefixes, 10.6))
-    events = sorted((2.8 * c + lag, i, c) for i, (_, lag) in enumerate(stages) for c in range(chunks))
-    share = -(-pairs // max(1, len(events) - 4))
-    share += share % 2
+    stages = ((scan_line, 0.0), (scan_lines, 6.0), (prefixes, 11.0))
+    events = sorted((3.2 * c + lag, i, c) for i, (_, lag) in enumerate(stages) for c in range(chunks))
     done = 0
     for place, (_, i, c) in enumerate(events):
-        want = min(pairs, share * (place + 1))
+        want = (pairs * (5, 7, 8)[min(place, 2)]) // 16 * 2
         if want > done:
             over_pairs(done, want, 2, intra)
             done = want
         stages[i][0](c)
+        if i == 0 and c + ahead < chunks:
+            state_out(c + ahead)
     for c in range(chunks):
         finish(c)
 
@@ -308,11 +348,13 @@
 
     loop_z(lambda zz: info_z(x * nz + zz, me).wait_send())
     loop_x(lambda xx: info_x(xx, x).wait_send())
+    for k in (1, 2):
+        when_later(k, lambda: send_ends(k).wait_send())
     for c in range(chunks):
         loop_z(lambda zz: send_state(c, zz, z).wait_send())
-        loop_x(lambda xx: send_total(c, xx, x).wait_send())
-        send_slice(c, 1).wait_send()
-        send_slice(c, 2).wait_send()
+        for k in (1, 2):
+            when_later(k, lambda: all_x(lambda xx: send_total(c, k, xx, x).wait_send()))
+        loop_x(lambda xx: send_total(c, 0, xx, x).wait_send())
         loop_x(lambda xx: send_carry(c, xx, x).wait_send())
         loop_z(lambda zz: send_prefix(c, zz, z).wait_send())
 
@@ -349,21 +391,18 @@
                 pltpu.VMEM((chunks, nz, HD, PAIR), BF16),
                 pltpu.VMEM((chunks, nz, HD, PAIR), BF16),
                 pltpu.VMEM((nz + 1, chunks, HD, PAIR), F32),
-                pltpu.VMEM((chunks, nx, rx, PAIR), F32),
-                pltpu.VMEM((chunks, nx, rx, PAIR), F32),
-                pltpu.VMEM((chunks, rx + 8, PAIR), F32),
-                pltpu.VMEM((chunks, rx + 8, PAIR), F32),
-                pltpu.VMEM((chunks, rx + 8, PAIR), F32),
+                pltpu.VMEM((chunks, 3, nx, rx, PAIR), F32),
+                pltpu.VMEM((nx, PAIR), F32),
+                pltpu.VMEM((2, nx, PAIR), F32),
                 pltpu.VMEM((chunks, nx, rx, PAIR), F32),
                 pltpu.VMEM((chunks, nx, rx, PAIR), F32),
                 pltpu.VMEM((chunks, nz, HD, PAIR), BF16),
                 pltpu.VMEM((chunks, nz, HD, PAIR), BF16),
-                pltpu.VMEM((8, PAIR), F32),
                 sem((5,)),
                 sem((nz,)), sem((nz,)), sem((nx,)), sem((nx,)),
                 sem((chunks, nz)), sem((chunks, nz)),
-                sem((chunks, nx)), sem((chunks, nx)),
-                sem((chunks, 2)), sem((chunks, 2)),
+                sem((chunks, 3, nx)), sem((chunks, 3, nx)),
+                pltpu.SemaphoreType.REGULAR((2,)), sem((2,)), sem((2,)),
                 sem((chunks, nx)), sem((chunks, nx)),
                 sem((chunks, nz)), sem((chunks, nz)),
             ],

time: 72.6 us -> 70 us (0.964)
  the two profiles are of different devices: /device:TPU:2 before, /device:TPU:112 now
where the time goes in v3:
time: 70 us; the launch traced here: 69.8 us
  Pallas kernels  68.3 us (98%)
  local copies, waits for them, and re-layouts  0.88 us (1%)
    pallas_call x1, Pallas kernels, local(): pl.pallas_call(functools.partial(kernel, nx, nz, nctx, tok), out_shape=ja...  68.3 us

profile of v3, /device:TPU:112, one launch (start us, length us, event | category | flops | bytes accessed | tf_op | source)
XLA Modules:
  0.0 69.8 jit_solution(7073754312542299399)
XLA Ops:
  0.7 68.3 %shard_map.64 = bf16[96,4096]{1,0:T(8,128)(2,1)S(1)} custom-call(bf16[96,4096]{1,0:T(8,128)(2,1)} %q_hbm.1, bf16[96,4096]{1,0:T(8,128)(2,1)} %k_hbm.1, bf16[96,4096]{1,0:T(8,128)(2,1)} %v_hbm.1, s32[1,96]{1,0:T(1,128)} %bitcast.3, f32[1,4096]{1,0:T(1,128)} %bitcast.2, f32[1]{0:T(128)S(6)} %copy.8.rate_ref), custom_call_target="tpu_custom_call" | custom-call | tf_op jit(solution)/shard_map/pallas_call | solution.py:373
  69.0 0.9 %copy.9 = bf16[96,4096]{1,0:T(8,128)(2,1)} copy(bf16[96,4096]{1,0:T(8,128)(2,1)S(1)} %shard_map.64) | data formatting | bytes 1572864

commit v4 on v3

--- a/solution.py
+++ b/solution.py
@@ -110,10 +110,6 @@
         for off in sorted(range(1, nz), key=lambda o: -min(o, nz - o)):
             body(on_line(off))
 
-    def every_x(body):
-        for off in sorted(range(nx), key=lambda o: -min(o, nx - o)):
-            body(on_column(off))
-
     def far_x(body):
         for off in sorted(range(1, nx), key=lambda o: -min(o, nx - o)):
             body(on_column(off))
@@ -196,7 +192,7 @@
         return pltpu.make_async_remote_copy(s_send.at[c, to], s_recv.at[c, frm], s_s.at[c, to], s_r.at[c, frm],
                                             device_id=dev(x, to), device_id_type=MESH)
 
-    ahead = 3
+    ahead = 2
 
     def state_out(c):
         far_z(lambda zz: send_state(c, zz, z).start())
@@ -247,9 +243,9 @@
             total = state
         line[nz, c] = total
         t_recv[c, 0, x] = line[nz, c, pl.ds(pl.multiple_of(x * rx, rx), rx)]
+        for k in (2, 1):
+            when_later(k, lambda: all_x(lambda xx: send_total(c, k, xx, x).start()))
         far_x(lambda xx: send_total(c, 0, xx, x).start())
-        for k in (1, 2):
-            when_later(k, lambda: every_x(lambda xx: send_total(c, k, xx, x).start()))
 
     def send_carry(c, to, frm):
         return pltpu.make_async_remote_copy(o_send.at[c, to], o_recv.at[c, frm], o_s.at[c, to], o_r.at[c, frm],

time: 70 us -> 68.5 us (0.979)
  the two profiles are of different devices: /device:TPU:112 before, /device:TPU:48 now
where the time goes in v4:
time: 68.5 us; the launch traced here: 68.3 us
  Pallas kernels  66.8 us (98%)
  local copies, waits for them, and re-layouts  0.88 us (1%)
    pallas_call x1, Pallas kernels, local(): pl.pallas_call(functools.partial(kernel, nx, nz, nctx, tok), out_shape=ja...  66.8 us

profile of v4, /device:TPU:48, one launch (start us, length us, event | category | flops | bytes accessed | tf_op | source)
XLA Modules:
  0.0 68.3 jit_solution(15916367044178369288)
XLA Ops:
  0.7 66.8 %shard_map.64 = bf16[96,4096]{1,0:T(8,128)(2,1)S(1)} custom-call(bf16[96,4096]{1,0:T(8,128)(2,1)} %q_hbm.1, bf16[96,4096]{1,0:T(8,128)(2,1)} %k_hbm.1, bf16[96,4096]{1,0:T(8,128)(2,1)} %v_hbm.1, s32[1,96]{1,0:T(1,128)} %bitcast.3, f32[1,4096]{1,0:T(1,128)} %bitcast.2, f32[1]{0:T(128)S(6)} %copy.8.rate_ref), custom_call_target="tpu_custom_call" | custom-call | tf_op jit(solution)/shard_map/pallas_call | solution.py:369
  67.5 0.9 %copy.9 = bf16[96,4096]{1,0:T(8,128)(2,1)} copy(bf16[96,4096]{1,0:T(8,128)(2,1)S(1)} %shard_map.64) | data formatting | bytes 1572864
